TPU v7x, 512 devices: a whole 4x4x16 slice. The times are simulated.
512 devices in a mesh: dp: 8 (over z_hi, y), shard: 64 (over x, z_lo, core).
Axes of the slice: x: 4, y: 4, z: 16 (z_hi: 2, z_lo: 8; z = z_hi * 8 + z_lo), core: 2. Of those that a mesh axis runs over, the one named last changes fastest.
Arguments:
- context: bfloat16 [8192, 4096], P('shard'), may hold values from -16 to 16
- projected: bfloat16 [8192, 4096], P('shard', 'dp'), may hold values from -6 to 6
- cotangent: bfloat16 [8192, 4096], P('shard', 'dp'), may hold values from -16 to 16
- modality: int32 [8192], P('shard'), may hold values from 0 to 2
- out_weight: bfloat16 [4096, 3, 4096], P('shard', None, 'dp'), may hold values from -0.09375 to 0.09375
- out_gain: float32 [3, 4096], P(None, 'dp'), may hold values from 0.25 to 1.75
Outputs:
- grad_context: bfloat16 [8192, 4096], P('shard', 'dp')
- grad_weight: float32 [4096, 3, 4096], P('shard', None, 'dp')
- grad_gain: float32 [3, 4096], P(None, 'dp')
All inputs are finite; a program needn't handle non-finite values.
Results may differ from a plain program's by a relative error of at most 0.0049.
Values may be sent and summed in bfloat16 or wider, within the bound.
No kernel may reach another device: no remote copies, remote signals or barrier semaphores. Data moves between devices by JAX's collectives and lax.ppermute only.
A program may use at most 64 MiB of HBM per device.

v0:
```python
import jax
import jax.numpy as jnp
from jax import lax
from jax.sharding import Mesh
from jax.sharding import PartitionSpec as P

D = 4096
DP = ("dp_0", "dp_1")
EPS = 1e-06


def from_everyone(shard, axis):
    count = lax.axis_size(axis)
    return lax.all_to_all(
        jnp.broadcast_to(shard[None], (count, *shard.shape)), axis, 0, 0, tiled=True
    )


def of_everyone(shard, axis):
    everything = from_everyone(shard, axis)
    return jnp.sum(everything, axis=0)


def packed_total(arrays, axis):
    ravelled, at, outs = (jnp.concatenate([a.reshape(-1) for a in arrays]), 0, [])
    total = of_everyone(ravelled, axis)
    for a in arrays:
        outs.append(total[at : at + a.size].reshape(a.shape))
        at += a.size
    return tuple(outs)


def sum_in_order(pieces, axes, order):
    lengths = [lax.axis_size(a) for a in axes]
    pieces = pieces.reshape(*lengths, *pieces.shape[1:])
    pieces = pieces.transpose(*order, *range(len(axes), pieces.ndim))
    pieces = pieces.reshape(-1, *pieces.shape[len(axes) :])
    for k in order:
        pieces = lax.psum_scatter(pieces, axes[k], scatter_dimension=0, tiled=True)
    return pieces[0]


def cut_along(shard, dim, count):
    lengths = shard.shape
    pieces = shard.reshape(*lengths[:dim], count, lengths[dim] // count, *lengths[dim + 1 :])
    return jnp.moveaxis(pieces, dim, 0)


def summed_rows(shard, axes, order, dim):
    count = lax.axis_size(axes)
    return sum_in_order(cut_along(shard, dim, count), axes, order)


def local(context, projected, cotangent, modality, out_weight, out_gain):
    towers = out_weight.shape[1]
    tower_ids = jnp.arange(towers, dtype=jnp.int32)
    onehot = (modality[:, None] == tower_ids[None, :]).astype(jnp.float32)
    proj_float = projected.astype(jnp.float32)
    cot_float = cotangent.astype(jnp.float32)
    gain_tok = jnp.dot(onehot, out_gain, precision=lax.Precision.HIGHEST)
    scaled = cot_float * gain_tok
    squares, raw_inner = packed_total(
        (
            jnp.sum(proj_float * proj_float, axis=1, keepdims=True),
            jnp.sum(scaled * proj_float, axis=1, keepdims=True),
        ),
        DP,
    )
    inverse_rms = lax.rsqrt(squares / D + EPS)
    normed = proj_float * inverse_rms
    inner = inverse_rms * raw_inner
    gain_terms = jnp.dot(onehot.T, cot_float * normed, precision=lax.Precision.HIGHEST)
    grad_gain = of_everyone(gain_terms, "shard")
    grad_proj = (inverse_rms * (scaled - normed * (inner / D))).astype(jnp.bfloat16)
    column_rows = lax.all_to_all(context, "shard", split_axis=1, concat_axis=0, tiled=True)
    row_count = out_weight.shape[0]
    piece_grad = lax.all_gather(grad_proj, "shard", axis=0, tiled=True)
    piece_ids = lax.all_gather(modality, "shard", axis=0, tiled=True)
    count = piece_grad.shape[0]
    piece_partial = jnp.zeros((count, row_count), jnp.float32)
    updated = []
    for member in range(towers):
        chosen = piece_ids[:, None] == member
        product = lax.dot_general(
            piece_grad,
            out_weight[:, member, :],
            (((1,), (1,)), ((), ())),
            preferred_element_type=jnp.float32,
        )
        piece_partial = piece_partial + chosen.astype(jnp.float32) * product
        masked = jnp.where(chosen, column_rows, jnp.zeros_like(column_rows))
        updated.append(
            lax.dot_general(
                masked, piece_grad, (((0,), (0,)), ((), ())), preferred_element_type=jnp.float32
            )
        )
    partial_value = piece_partial
    weight_accs, partial_value = (tuple(updated), partial_value)
    grad_weight = jnp.stack(weight_accs, axis=1)
    shard_count = lax.axis_size("shard")
    replica_count = lax.axis_size(DP)
    tok_here = grad_proj.shape[0]
    sub_rows = tok_here // replica_count
    grouped = partial_value.reshape(shard_count, replica_count, sub_rows, row_count)
    reduced = summed_rows(grouped, DP, (1, 0), 1).astype(jnp.bfloat16)
    reduced = reduced.reshape(shard_count, sub_rows, row_count)
    spread = lax.all_to_all(reduced, "shard", split_axis=0, concat_axis=2, tiled=True)
    settled = lax.all_to_all(spread, DP, split_axis=2, concat_axis=1, tiled=True)
    grad_context = settled.reshape(tok_here, settled.shape[2])
    return (grad_context, grad_weight, grad_gain)


def solution(mesh):
    finer = Mesh(mesh.devices.reshape(2, 4, mesh.shape["shard"]), ("dp_0", "dp_1", "shard"))
    return jax.shard_map(
        local,
        mesh=finer,
        in_specs=(
            P("shard", None),
            P("shard", DP),
            P("shard", DP),
            P("shard"),
            P("shard", None, DP),
            P(None, DP),
        ),
        out_specs=(P("shard", DP), P("shard", None, DP), P(None, DP)),
        check_vma=False,
    )
```

profile of v0, /device:TPU:32, one launch (start us, length us, event | category | flops | bytes accessed | tf_op | source)
XLA Modules:
  0.0 406.7 jit_solution(18081353275957798756)
XLA Ops:
  7.9 1.4 fusion.16
  9.3 31.5 %all_to_all.63 = f32[8,1,256]{2,1,0:T(1,128)S(1)} all-to-all(f32[8,1,256]{2,1,0:T(1,128)S(1)} %broadcast_in_dim.35), channel_id=1, replica_groups=mesh['dp_0'=2,'dp_1'=4,'shard'=64] {'dp_0','dp_1'}, dimensions={0} | all-to-all | bytes 16384 | tf_op jit(solution)/shard_map/all_to_all | solution.py:14
  40.9 1.7 fusion.14
  42.6 113.4 %all-gather = s32[64,1,128]{2,1,0:T(1,128)S(1)} all-gather(s32[1,1,128]{2,1,0:T(1,128)} %bitcast.89), channel_id=1, replica_groups=mesh['dp_0'=2,'dp_1'=4,'shard'=64] {'shard'}, dimensions={0}, use_global_device_ids=true | all-gather | bytes 33280 | tf_op jit(solution)/shard_map/all_gather | solution.py:78
  156.0 1.3 fusion.15
  157.3 0.9 broadcast_in_dim.39
  158.2 10.1 %all-to-all-start.4 = ((f32[64,3,512]{2,1,0:T(4,128)}), f32[64,3,512]{2,1,0:T(4,128)S(1)}, u32[]{:S(2)}, u32[]{:S(2)}) async-start(f32[64,3,512]{2,1,0:T(4,128)} %broadcast_in_dim.39), calls=%async_computation.6 | async-start | bytes 1048576 | tf_op jit(solution)/shard_map/all_to_all | solution.py:14
  168.3 6.2 %convolution_multiply_fusion = f32[8192,64]{0,1:T(8,128)S(1)} fusion(bf16[8192,512]{1,0:T(8,128)(2,1)} %all-gather.3.cloned.1.call-done, f32[8192]{0:T(1024)S(1)} %get-tuple-element.11, bf16[64,3,512]{2,0,1:T(8,128)(2,1)} %param.10), kind=kOutput, calls=%fused_computation | convolution fusion | flops 537395200 | bytes 10584064 | tf_op jit(solution)/shard_map/dot_general | solution.py:84
  174.5 2.6 convolution_multiply_fusion.1
  177.2 2.6 fusion.1
  179.8 2.7 copy.46
  182.5 4.5 %copy.47 = f32[2,4,64,1,16,64]{5,4,2,0,1,3:T(8,128)} copy(f32[2,4,64,1,16,64]{5,4,1,0,2,3:T(8,128)} %bitcast.81) | data formatting | bytes 4194304 | tf_op jit(solution)/shard_map/reshape | solution.py:35
  187.1 1.2 copy-done.2
  188.3 1.3 copy.52
  189.5 6.7 %all-to-all-done.4 = f32[64,3,512]{2,1,0:T(4,128)S(1)} async-done(((f32[64,3,512]{2,1,0:T(4,128)}), f32[64,3,512]{2,1,0:T(4,128)S(1)}, u32[]{:S(2)}, u32[]{:S(2)}) %all-to-all-start.4) | async-done | bytes 393248 | tf_op jit(solution)/shard_map/all_to_all | solution.py:14
  196.3 9.1 %all-to-all-start.3 = ((bf16[128,64,64]{0,2,1:T(8,128)(2,1)}), bf16[128,64,64]{0,2,1:T(8,128)(2,1)S(1)}, u32[]{:S(2)}, u32[]{:S(2)}) async-start(bf16[128,64,64]{0,2,1:T(8,128)(2,1)} %bitcast.20), calls=%async_computation.5 | async-start | bytes 2097152 | tf_op jit(solution)/shard_map/all_to_all | solution.py:75
  205.5 33.3 %reduce-scatter.3.cloned.1.call-done = f32[2,64,1,16,64]{4,3,1,0,2:T(8,128)} async-done(((f32[8,64,1,16,64]{4,3,1,0,2:T(8,128)}), f32[2,64,1,16,64]{4,3,1,0,2:T(8,128)}) %reduce-scatter.3.cloned.1.call-update) | async-done | bytes 524304 | tf_op jit(solution)/shard_map/reduce_scatter | solution.py:39
  239.5 15.5 %all-to-all-done.3 = bf16[128,64,64]{0,2,1:T(8,128)(2,1)S(1)} async-done(((bf16[128,64,64]{0,2,1:T(8,128)(2,1)}), bf16[128,64,64]{0,2,1:T(8,128)(2,1)S(1)}, u32[]{:S(2)}, u32[]{:S(2)}) %all-to-all-start.3) | async-done | bytes 1048608 | tf_op jit(solution)/shard_map/all_to_all | solution.py:75
  255.1 5.3 %convolution_bitcast_fusion = f32[64,1,512]{2,0,1:T(8,128)S(1)} fusion(bf16[8192,512]{1,0:T(8,128)(2,1)} %all-gather.3.cloned.1.call-done, pred[8192]{0:T(1024)(128)(4,1)S(1)} %get-tuple-element.12, bf16[128,64,64]{0,2,1:T(8,128)(2,1)S(1)} %all-to-all-done.3), kind=kOutput, calls=%fused_computation.6 | convolution fusion | flops 537395200 | bytes 9576448 | tf_op jit(solution)/shard_map/dot_general | solution.py:93
  260.3 46.1 %reduce-scatter.5.cloned.1.call-done = f32[1,64,1,16,64]{4,3,1,0,2:T(8,128)} async-done(((f32[2,64,1,16,64]{4,3,1,0,2:T(8,128)}), f32[1,64,1,16,64]{4,3,1,0,2:T(8,128)}) %reduce-scatter.5.cloned.1.call-update) | async-done | bytes 262160 | tf_op jit(solution)/shard_map/reduce_scatter | solution.py:39
  306.4 1.1 convert_bitcast_fusion
  308.3 14.9 %all-to-all-start.1 = ((bf16[64,2,512]{2,1,0:T(2,128)(2,1)}), bf16[64,2,512]{2,1,0:T(2,128)(2,1)S(1)}, u32[]{:S(2)}, u32[]{:S(2)}) async-start(bf16[64,2,512]{2,1,0:T(2,128)(2,1)} %reshape.65), calls=%async_computation.3 | async-start | bytes 262144 | tf_op jit(solution)/shard_map/all_to_all | solution.py:107
  323.2 4.9 %convolution_bitcast_fusion.1 = f32[64,1,512]{2,0,1:T(8,128)S(1)} fusion(bf16[8192,512]{1,0:T(8,128)(2,1)} %all-gather.3.cloned.1.call-done, pred[8192]{0:T(1024)(128)(4,1)S(1)} %get-tuple-element.14, bf16[128,64,64]{0,2,1:T(8,128)(2,1)S(1)} %all-to-all-done.3), kind=kOutput, calls=%fused_computation.7 | convolution fusion | flops 537395200 | bytes 9576448 | tf_op jit(solution)/shard_map/dot_general | solution.py:93
  328.1 8.7 %all-to-all-done.1 = bf16[64,2,512]{2,1,0:T(2,128)(2,1)S(1)} async-done(((bf16[64,2,512]{2,1,0:T(2,128)(2,1)}), bf16[64,2,512]{2,1,0:T(2,128)(2,1)S(1)}, u32[]{:S(2)}, u32[]{:S(2)}) %all-to-all-start.1) | async-done | bytes 131104 | tf_op jit(solution)/shard_map/all_to_all | solution.py:107
  337.4 2.7 copy.49
  340.7 23.5 %reduce.1 = bf16[4096,16]{1,0:T(8,128)(2,1)} reduce(bf16[4096,1,16]{2,1,0:T(2,128)(2,1)S(1)} %bitcast.82, bf16[]{:T(256)} %broadcast.57), dimensions={1}, to_apply=%bitcast.58.reduce_sub_computation | reduce | bytes 262146
  364.2 3.1 reshape.67
  367.3 10.1 %all-to-all-start.2 = ((bf16[8,2,4096]{2,1,0:T(2,128)(2,1)}), bf16[8,2,4096]{2,1,0:T(2,128)(2,1)S(1)}, u32[]{:S(2)}, u32[]{:S(2)}) async-start(bf16[8,2,4096]{2,1,0:T(2,128)(2,1)} %reshape.67), calls=%async_computation.4 | async-start | bytes 262144 | tf_op jit(solution)/shard_map/all_to_all | solution.py:108
  377.3 4.9 %convolution_bitcast_fusion.2 = f32[64,1,512]{2,0,1:T(8,128)S(1)} fusion(bf16[8192,512]{1,0:T(8,128)(2,1)} %all-gather.3.cloned.1.call-done, pred[8192]{0:T(1024)(128)(4,1)S(1)} %get-tuple-element.6, bf16[128,64,64]{0,2,1:T(8,128)(2,1)S(1)} %all-to-all-done.3), kind=kOutput, calls=%fused_computation.8 | convolution fusion | flops 537395200 | bytes 9576448 | tf_op jit(solution)/shard_map/dot_general | solution.py:93
  383.0 12.6 %all-to-all-done.2 = bf16[8,2,4096]{2,1,0:T(2,128)(2,1)S(1)} async-done(((bf16[8,2,4096]{2,1,0:T(2,128)(2,1)}), bf16[8,2,4096]{2,1,0:T(2,128)(2,1)S(1)}, u32[]{:S(2)}, u32[]{:S(2)}) %all-to-all-start.2) | async-done | bytes 131104 | tf_op jit(solution)/shard_map/all_to_all | solution.py:108
  395.6 1.8 reshape.68
  397.4 2.0 copy.50
  (29 shorter events, 5.1 us)
Async XLA Ops:
  7.2 0.7 copy-start
  7.2 161.1 %all-gather.3.cloned.1.call-start = ((), (), s32[]{:S(2)}) async-start(), calls=%async_computation.7 | async-start | bytes 8519680 | tf_op jit(solution)/shard_map/all_gather | solution.py:77
  158.2 38.1 %all-to-all-start.4 = ((f32[64,3,512]{2,1,0:T(4,128)}), f32[64,3,512]{2,1,0:T(4,128)S(1)}, u32[]{:S(2)}, u32[]{:S(2)}) async-start(f32[64,3,512]{2,1,0:T(4,128)} %broadcast_in_dim.39), calls=%async_computation.6 | async-start | bytes 1048576 | tf_op jit(solution)/shard_map/all_to_all | solution.py:14
  168.2 70.5 %reduce-scatter.3.cloned.1.call-start = ((), (), s32[]{:S(2)}) async-start(), calls=%async_computation.8 | async-start | bytes 5242880 | tf_op jit(solution)/shard_map/reduce_scatter | solution.py:39
  168.3 6.2 %copy-start.1 = (bf16[8192,512]{1,0:T(8,128)(2,1)S(1)}, bf16[8192,512]{1,0:T(8,128)(2,1)}, u32[]{:S(2)}) copy-start(bf16[8192,512]{1,0:T(8,128)(2,1)} %all-gather.3.cloned.1.call-done) | copy-start | bytes 25165828
  168.3 6.2 %copy-start.3 = (bf16[64,3,512]{2,0,1:T(8,128)(2,1)S(1)}, bf16[64,3,512]{2,0,1:T(8,128)(2,1)}, u32[]{:S(2)}) copy-start(bf16[64,3,512]{2,0,1:T(8,128)(2,1)} %param.10) | copy-start | bytes 589828
  187.0 1.2 copy-start.2
  196.3 58.8 %all-to-all-start.3 = ((bf16[128,64,64]{0,2,1:T(8,128)(2,1)}), bf16[128,64,64]{0,2,1:T(8,128)(2,1)S(1)}, u32[]{:S(2)}, u32[]{:S(2)}) async-start(bf16[128,64,64]{0,2,1:T(8,128)(2,1)} %bitcast.20), calls=%async_computation.5 | async-start | bytes 2097152 | tf_op jit(solution)/shard_map/all_to_all | solution.py:75
  205.4 101.0 %reduce-scatter.5.cloned.1.call-start = ((), (), s32[]{:S(2)}) async-start(), calls=%async_computation.9 | async-start | bytes 1572864 | tf_op jit(solution)/shard_map/reduce_scatter | solution.py:39
  308.3 28.5 %all-to-all-start.1 = ((bf16[64,2,512]{2,1,0:T(2,128)(2,1)}), bf16[64,2,512]{2,1,0:T(2,128)(2,1)S(1)}, u32[]{:S(2)}, u32[]{:S(2)}) async-start(bf16[64,2,512]{2,1,0:T(2,128)(2,1)} %reshape.65), calls=%async_computation.3 | async-start | bytes 262144 | tf_op jit(solution)/shard_map/all_to_all | solution.py:107
  367.3 28.3 %all-to-all-start.2 = ((bf16[8,2,4096]{2,1,0:T(2,128)(2,1)}), bf16[8,2,4096]{2,1,0:T(2,128)(2,1)S(1)}, u32[]{:S(2)}, u32[]{:S(2)}) async-start(bf16[8,2,4096]{2,1,0:T(2,128)(2,1)} %reshape.67), calls=%async_computation.4 | async-start | bytes 262144 | tf_op jit(solution)/shard_map/all_to_all | solution.py:108
Sparse Core Ops, SparseCore 0:
  42.7 119.8 all-gather.2
  187.2 51.5 reduce-scatter.2
  241.6 64.7 reduce-scatter.4
where the time goes:
time: 408 us; the launch traced here: 407 us
  blocking collectives  145 us (36%)
  waiting for transfers between devices  123 us (30%)
  starting transfers between devices  44.3 us (11%)
  matrix products  29.2 us (7%)
  other arithmetic  27.8 us (7%)
  local copies, waits for them, and re-layouts  23.6 us (6%)
  between operations  13.9 us (3%)
    all_gather x1, blocking collectives, local(): piece_ids = lax.all_gather(modality, 'shard', axis=0, tiled=True)  113 us
    reduce_scatter x2, waiting for transfers between devices, sum_in_order(): pieces = lax.psum_scatter(pieces, axes[k], scatter_dimension=0, tiled=True)  79.4 us
    all_to_all x1, blocking collectives, from_everyone(): lax.all_to_all(jnp.broadcast_to(shard[None], (count, *shard.shape)), axis...  31.5 us
    unnamed x1, other arithmetic  23.5 us
    all_to_all x1, waiting for transfers between devices, local(): lax.all_to_all(context, 'shard', split_axis=1, concat_axis=0, tiled=True)  15.5 us
    dot_general x3, matrix products, local(): lax.dot_general(masked, piece_grad, (((0,), (0,)), ((), ())), preferred_e...  15.1 us
    all_to_all x1, starting transfers between devices, local(): lax.all_to_all(reduced, 'shard', split_axis=0, concat_axis=2, tiled=True)  14.9 us
    all_to_all x1, waiting for transfers between devices, local(): lax.all_to_all(spread, DP, split_axis=2, concat_axis=1, tiled=True)  12.6 us
  transfers between devices with their start and end apart: 7, of which 6 were waited for; matrix products, arithmetic and copies ran while one was open for 10% of the time, Pallas kernels for 0%

commit v1 on v0

--- a/solution.py
+++ b/solution.py
@@ -72,7 +72,12 @@
     gain_terms = jnp.dot(onehot.T, cot_float * normed, precision=lax.Precision.HIGHEST)
     grad_gain = of_everyone(gain_terms, "shard")
     grad_proj = (inverse_rms * (scaled - normed * (inner / D))).astype(jnp.bfloat16)
-    column_rows = lax.all_to_all(context, "shard", split_axis=1, concat_axis=0, tiled=True)
+    column_rows = jnp.concatenate(
+        lax.all_to_all(
+            jnp.stack(jnp.split(context, lax.axis_size("shard"), axis=1)), "shard", 0, 0
+        ),
+        axis=0,
+    )
     row_count = out_weight.shape[0]
     piece_grad = lax.all_gather(grad_proj, "shard", axis=0, tiled=True)
     piece_ids = lax.all_gather(modality, "shard", axis=0, tiled=True)

time: 408 us -> 452 us (1.11)
  local copies, waits for them, and re-layouts: 23.6 us -> 68.2 us
    unnamed x15 -> x147, local copies, waits for them, and re-layouts: 9.67 us -> 51 us
  transfers between devices with their start and end apart: 7 -> 7, of which waited for: 6 -> 6; matrix products, arithmetic and copies ran while one was open for 10% -> 19% of each run, Pallas kernels for 0% -> 0%
where the time goes in v1:
time: 452 us; the launch traced here: 451 us
  blocking collectives  145 us (32%)
  waiting for transfers between devices  123 us (27%)
  local copies, waits for them, and re-layouts  68.2 us (15%)
  starting transfers between devices  44.4 us (10%)
  matrix products  28.2 us (6%)
  other arithmetic  27.8 us (6%)
  between operations  14.6 us (3%)
    all_gather x1, blocking collectives, local(): piece_ids = lax.all_gather(modality, 'shard', axis=0, tiled=True)  113 us
    reduce_scatter x2, waiting for transfers between devices, sum_in_order(): pieces = lax.psum_scatter(pieces, axes[k], scatter_dimension=0, tiled=True)  79.1 us
    unnamed x147, local copies, waits for them, and re-layouts  51 us
    all_to_all x1, blocking collectives, from_everyone(): lax.all_to_all(jnp.broadcast_to(shard[None], (count, *shard.shape)), axis...  31.5 us
    unnamed x1, other arithmetic  23.5 us
    all_to_all x1, waiting for transfers between devices, local(): lax.all_to_all(jnp.stack(jnp.split(context, lax.axis_size('shard'), axis=...  15.6 us
    dot_general x3, matrix products, local(): lax.dot_general(masked, piece_grad, (((0,), (0,)), ((), ())), preferred_e...  15.1 us
    all_to_all x1, starting transfers between devices, local(): lax.all_to_all(reduced, 'shard', split_axis=0, concat_axis=2, tiled=True)  15.1 us
  transfers between devices with their start and end apart: 7, of which 6 were waited for; matrix products, arithmetic and copies ran while one was open for 19% of the time, Pallas kernels for 0%

profile of v1, /device:TPU:32, one launch (start us, length us, event | category | flops | bytes accessed | tf_op | source)
XLA Modules:
  0.0 451.2 jit_solution(15223505715291028042)
XLA Ops:
  7.9 1.4 fusion.16
  9.3 31.5 %all_to_all.49 = f32[8,1,256]{2,1,0:T(1,128)S(1)} all-to-all(f32[8,1,256]{2,1,0:T(1,128)S(1)} %broadcast_in_dim.35), channel_id=1, replica_groups=mesh['dp_0'=2,'dp_1'=4,'shard'=64] {'dp_0','dp_1'}, dimensions={0} | all-to-all | bytes 16384 | tf_op jit(solution)/shard_map/all_to_all | solution.py:14
  40.9 1.7 fusion.14
  42.6 1.0 fusion.36
  44.3 1.3 fusion.35
  51.6 113.3 %all-gather = s32[64,1,128]{2,1,0:T(1,128)S(1)} all-gather(s32[1,1,128]{2,1,0:T(1,128)S(1)} %bitcast.215), channel_id=1, replica_groups=mesh['dp_0'=2,'dp_1'=4,'shard'=64] {'shard'}, dimensions={0}, use_global_device_ids=true | all-gather | bytes 33280 | tf_op jit(solution)/shard_map/all_gather | solution.py:83
  201.9 0.9 broadcast_in_dim.39
  202.8 10.0 %all-to-all-start.4 = ((f32[64,3,512]{2,1,0:T(4,128)}), f32[64,3,512]{2,1,0:T(4,128)S(1)}, u32[]{:S(2)}, u32[]{:S(2)}) async-start(f32[64,3,512]{2,1,0:T(4,128)} %broadcast_in_dim.39), calls=%async_computation.6 | async-start | bytes 1048576 | tf_op jit(solution)/shard_map/all_to_all | solution.py:14
  212.9 6.2 %convolution_multiply_fusion = f32[8192,64]{0,1:T(8,128)S(1)} fusion(bf16[8192,512]{1,0:T(8,128)(2,1)} %all-gather.3.cloned.1.call-done, f32[8192]{0:T(1024)S(1)} %get-tuple-element.75, bf16[64,3,512]{2,0,1:T(8,128)(2,1)S(1)} %copy-done.4), kind=kOutput, calls=%fused_computation | convolution fusion | flops 537395200 | bytes 10584064 | tf_op jit(solution)/shard_map/dot_general | solution.py:89
  219.1 2.6 convolution_multiply_fusion.1
  221.7 2.6 fusion.1
  224.3 2.7 copy.241
  227.0 4.6 %copy.242 = f32[2,4,64,1,16,64]{5,4,2,0,1,3:T(8,128)} copy(f32[2,4,64,1,16,64]{5,4,1,0,2,3:T(8,128)} %bitcast.207) | data formatting | bytes 4194304 | tf_op jit(solution)/shard_map/reshape | solution.py:35
  233.6 7.2 %all-to-all-done.4 = f32[64,3,512]{2,1,0:T(4,128)S(1)} async-done(((f32[64,3,512]{2,1,0:T(4,128)}), f32[64,3,512]{2,1,0:T(4,128)S(1)}, u32[]{:S(2)}, u32[]{:S(2)}) %all-to-all-start.4) | async-done | bytes 393248 | tf_op jit(solution)/shard_map/all_to_all | solution.py:14
  240.8 9.1 %all-to-all-start.3 = ((bf16[64,128,64]{1,2,0:T(8,128)(2,1)}), bf16[64,128,64]{1,2,0:T(8,128)(2,1)S(1)}, u32[]{:S(2)}, u32[]{:S(2)}) async-start(bf16[64,128,64]{1,2,0:T(8,128)(2,1)} %constant_dynamic-update-slice_fusion), calls=%async_computation.5 | async-start | bytes 2097152 | tf_op jit(solution)/shard_map/all_to_all | solution.py:76
  250.2 33.1 %reduce-scatter.3.cloned.1.call-done = f32[2,64,1,16,64]{4,3,1,0,2:T(8,128)} async-done(((f32[8,64,1,16,64]{4,3,1,0,2:T(8,128)}), f32[2,64,1,16,64]{4,3,1,0,2:T(8,128)}) %reduce-scatter.3.cloned.1.call-update) | async-done | bytes 524304 | tf_op jit(solution)/shard_map/reduce_scatter | solution.py:39
  284.0 15.6 %all-to-all-done.3 = bf16[64,128,64]{1,2,0:T(8,128)(2,1)S(1)} async-done(((bf16[64,128,64]{1,2,0:T(8,128)(2,1)}), bf16[64,128,64]{1,2,0:T(8,128)(2,1)S(1)}, u32[]{:S(2)}, u32[]{:S(2)}) %all-to-all-start.3) | async-done | bytes 1048608 | tf_op jit(solution)/shard_map/all_to_all | solution.py:76
  299.6 5.3 %convolution_bitcast_fusion.2 = f32[64,1,512]{2,0,1:T(8,128)S(1)} fusion(bf16[8192,512]{1,0:T(8,128)(2,1)} %all-gather.3.cloned.1.call-done, pred[8192]{0:T(1024)(128)(4,1)S(1)} %get-tuple-element.6, bf16[64,128,64]{1,2,0:T(8,128)(2,1)S(1)} %all-to-all-done.3), kind=kOutput, calls=%fused_computation.8 | convolution fusion | flops 537395200 | bytes 9576448 | tf_op jit(solution)/shard_map/dot_general | solution.py:98
  304.9 46.0 %reduce-scatter.5.cloned.1.call-done = f32[1,64,1,16,64]{4,3,1,0,2:T(8,128)} async-done(((f32[2,64,1,16,64]{4,3,1,0,2:T(8,128)}), f32[1,64,1,16,64]{4,3,1,0,2:T(8,128)}) %reduce-scatter.5.cloned.1.call-update) | async-done | bytes 262160 | tf_op jit(solution)/shard_map/reduce_scatter | solution.py:39
  350.9 1.1 convert_bitcast_fusion
  352.0 0.9 reshape.66
  352.9 15.1 %all-to-all-start.1 = ((bf16[64,2,512]{2,1,0:T(2,128)(2,1)}), bf16[64,2,512]{2,1,0:T(2,128)(2,1)S(1)}, u32[]{:S(2)}, u32[]{:S(2)}) async-start(bf16[64,2,512]{2,1,0:T(2,128)(2,1)} %reshape.66), calls=%async_computation.3 | async-start | bytes 262144 | tf_op jit(solution)/shard_map/all_to_all | solution.py:112
  368.0 4.9 %convolution_bitcast_fusion.1 = f32[64,1,512]{2,0,1:T(8,128)S(1)} fusion(bf16[8192,512]{1,0:T(8,128)(2,1)} %all-gather.3.cloned.1.call-done, pred[8192]{0:T(1024)(128)(4,1)S(1)} %get-tuple-element.78, bf16[64,128,64]{1,2,0:T(8,128)(2,1)S(1)} %all-to-all-done.3), kind=kOutput, calls=%fused_computation.7 | convolution fusion | flops 537395200 | bytes 9576448 | tf_op jit(solution)/shard_map/dot_general | solution.py:98
  372.9 8.7 %all-to-all-done.1 = bf16[64,2,512]{2,1,0:T(2,128)(2,1)S(1)} async-done(((bf16[64,2,512]{2,1,0:T(2,128)(2,1)}), bf16[64,2,512]{2,1,0:T(2,128)(2,1)S(1)}, u32[]{:S(2)}, u32[]{:S(2)}) %all-to-all-start.1) | async-done | bytes 131104 | tf_op jit(solution)/shard_map/all_to_all | solution.py:112
  382.2 2.7 copy.244
  385.4 23.5 %reduce.1 = bf16[4096,16]{1,0:T(8,128)(2,1)} reduce(bf16[4096,1,16]{2,1,0:T(2,128)(2,1)S(1)} %bitcast.208, bf16[]{:T(256)} %broadcast.57), dimensions={1}, to_apply=%bitcast.184.reduce_sub_computation | reduce | bytes 262146
  408.9 3.1 reshape.68
  412.0 9.8 %all-to-all-start.2 = ((bf16[8,2,4096]{2,1,0:T(2,128)(2,1)}), bf16[8,2,4096]{2,1,0:T(2,128)(2,1)S(1)}, u32[]{:S(2)}, u32[]{:S(2)}) async-start(bf16[8,2,4096]{2,1,0:T(2,128)(2,1)} %reshape.68), calls=%async_computation.4 | async-start | bytes 262144 | tf_op jit(solution)/shard_map/all_to_all | solution.py:113
  421.8 4.9 %convolution_bitcast_fusion = f32[64,1,512]{2,0,1:T(8,128)S(1)} fusion(bf16[8192,512]{1,0:T(8,128)(2,1)} %all-gather.3.cloned.1.call-done, pred[8192]{0:T(1024)(128)(4,1)S(1)} %get-tuple-element.76, bf16[64,128,64]{1,2,0:T(8,128)(2,1)S(1)} %all-to-all-done.3), kind=kOutput, calls=%fused_computation.6 | convolution fusion | flops 537395200 | bytes 9576448 | tf_op jit(solution)/shard_map/dot_general | solution.py:98
  427.5 12.6 %all-to-all-done.2 = bf16[8,2,4096]{2,1,0:T(2,128)(2,1)S(1)} async-done(((bf16[8,2,4096]{2,1,0:T(2,128)(2,1)}), bf16[8,2,4096]{2,1,0:T(2,128)(2,1)S(1)}, u32[]{:S(2)}, u32[]{:S(2)}) %all-to-all-start.2) | async-done | bytes 131104 | tf_op jit(solution)/shard_map/all_to_all | solution.py:113
  440.1 1.8 reshape.69
  441.9 2.0 copy.245
  (166 shorter events, 49.5 us)
Async XLA Ops:
  7.2 0.7 copy-start
  7.2 44.4 %copy-start.6 = (s32[128]{0:T(128)S(1)}, s32[128]{0:T(128)}, u32[]{:S(2)}) copy-start(s32[128]{0:T(128)} %param.9) | copy-start | bytes 1540
  7.2 40.3 %copy-start.2 = (bf16[128,4096]{1,0:T(8,128)(2,1)S(1)}, bf16[128,4096]{1,0:T(8,128)(2,1)}, u32[]{:S(2)}) copy-start(bf16[128,4096]{1,0:T(8,128)(2,1)} %param.6) | copy-start | bytes 3145732
  7.2 205.7 %all-gather.3.cloned.1.call-start = ((), (), s32[]{:S(2)}) async-start(), calls=%async_computation.7 | async-start | bytes 8519680 | tf_op jit(solution)/shard_map/all_gather | solution.py:82
  44.3 157.3 %copy-start.3 = (bf16[128,512]{1,0:T(8,128)(2,1)S(1)}, bf16[128,512]{1,0:T(8,128)(2,1)}, u32[]{:S(2)}) copy-start(bf16[128,512]{1,0:T(8,128)(2,1)} %param.7) | copy-start | bytes 393220
  44.3 157.3 %copy-start.5 = (bf16[128,512]{1,0:T(8,128)(2,1)S(1)}, bf16[128,512]{1,0:T(8,128)(2,1)}, u32[]{:S(2)}) copy-start(bf16[128,512]{1,0:T(8,128)(2,1)} %param.8) | copy-start | bytes 393220
  47.5 165.4 %copy-start.4 = (bf16[64,3,512]{2,0,1:T(8,128)(2,1)S(1)}, bf16[64,3,512]{2,0,1:T(8,128)(2,1)}, u32[]{:S(2)}) copy-start(bf16[64,3,512]{2,0,1:T(8,128)(2,1)} %param.10) | copy-start | bytes 589828
  202.8 38.0 %all-to-all-start.4 = ((f32[64,3,512]{2,1,0:T(4,128)}), f32[64,3,512]{2,1,0:T(4,128)S(1)}, u32[]{:S(2)}, u32[]{:S(2)}) async-start(f32[64,3,512]{2,1,0:T(4,128)} %broadcast_in_dim.39), calls=%async_computation.6 | async-start | bytes 1048576 | tf_op jit(solution)/shard_map/all_to_all | solution.py:14
  212.8 70.5 %reduce-scatter.3.cloned.1.call-start = ((), (), s32[]{:S(2)}) async-start(), calls=%async_computation.8 | async-start | bytes 5242880 | tf_op jit(solution)/shard_map/reduce_scatter | solution.py:39
  212.9 6.2 %copy-start.1 = (bf16[8192,512]{1,0:T(8,128)(2,1)S(1)}, bf16[8192,512]{1,0:T(8,128)(2,1)}, u32[]{:S(2)}) copy-start(bf16[8192,512]{1,0:T(8,128)(2,1)} %all-gather.3.cloned.1.call-done) | copy-start | bytes 25165828
  240.8 58.8 %all-to-all-start.3 = ((bf16[64,128,64]{1,2,0:T(8,128)(2,1)}), bf16[64,128,64]{1,2,0:T(8,128)(2,1)S(1)}, u32[]{:S(2)}, u32[]{:S(2)}) async-start(bf16[64,128,64]{1,2,0:T(8,128)(2,1)} %constant_dynamic-update-slice_fusion), calls=%async_computation.5 | async-start | bytes 2097152 | tf_op jit(solution)/shard_map/all_to_all | solution.py:76
  250.0 100.9 %reduce-scatter.5.cloned.1.call-start = ((), (), s32[]{:S(2)}) async-start(), calls=%async_computation.9 | async-start | bytes 1572864 | tf_op jit(solution)/shard_map/reduce_scatter | solution.py:39
  352.9 28.7 %all-to-all-start.1 = ((bf16[64,2,512]{2,1,0:T(2,128)(2,1)}), bf16[64,2,512]{2,1,0:T(2,128)(2,1)S(1)}, u32[]{:S(2)}, u32[]{:S(2)}) async-start(bf16[64,2,512]{2,1,0:T(2,128)(2,1)} %reshape.66), calls=%async_computation.3 | async-start | bytes 262144 | tf_op jit(solution)/shard_map/all_to_all | solution.py:112
  412.0 28.1 %all-to-all-start.2 = ((bf16[8,2,4096]{2,1,0:T(2,128)(2,1)}), bf16[8,2,4096]{2,1,0:T(2,128)(2,1)S(1)}, u32[]{:S(2)}, u32[]{:S(2)}) async-start(bf16[8,2,4096]{2,1,0:T(2,128)(2,1)} %reshape.68), calls=%async_computation.4 | async-start | bytes 262144 | tf_op jit(solution)/shard_map/all_to_all | solution.py:113
Sparse Core Ops, SparseCore 0:
  42.7 119.1 all-gather.2
  231.7 51.5 reduce-scatter.2
  286.1 64.7 reduce-scatter.4
